TPU v7x, 32 devices: a whole 2x2x4 slice. The times are simulated.
32 devices in a mesh: parts: 2 (over x), ctx: 16 (over z, y, core).
Axes of the slice: x: 2, y: 2, z: 4, core: 2. Of those that a mesh axis runs over, the one named last changes fastest.
Arguments:
- query_proj: bfloat16 [4096, 4096], P(('parts', 'ctx')), parts along dimension 0, may hold values from -6 to 6
- key_proj: bfloat16 [4096, 4096], P(('parts', 'ctx')), parts along dimension 0, may hold values from -6 to 6
- value_proj: bfloat16 [4096, 4096], P(('parts', 'ctx')), parts along dimension 0, may hold values from -6 to 6
- cotangent: bfloat16 [4096, 2048], P(('parts', 'ctx')), parts along dimension 0, may hold values from -6 to 6
- out_weight: bfloat16 [4096, 2048], P('ctx'), may hold values from -0.125 to 0.125
- filters: float32 [256, 2048], P('ctx'), may hold values from -1.2 to 1.2
Outputs:
- query_grad: float32 [4096, 4096], P(('parts', 'ctx')), parts along dimension 0
- key_grad: float32 [4096, 4096], P(('parts', 'ctx')), parts along dimension 0
- value_grad: float32 [4096, 4096], P(('parts', 'ctx')), parts along dimension 0
- filter_grad: float32 [512, 2048], P(('parts', 'ctx')), parts along dimension 0
There are 2 independent parts, one for each index of `parts`. A program takes and returns all parts, laid end to end along the dimension named above; an argument that names none is the same for every part. Nothing has to cross between parts.
All inputs are finite; a program needn't handle non-finite values.
Results may differ from a plain program's by a relative error of at most 0.005.
Values may be sent and summed in bfloat16 or wider, within the bound.
No kernel may reach another device: no remote copies, remote signals or barrier semaphores. Data moves between devices by JAX's collectives and lax.ppermute only.
A program may use at most 192 MiB of HBM per device.

v0:
```python
import math

import jax
import jax.numpy as jnp
from jax import lax
from jax.sharding import PartitionSpec as P

inner_len = 128


def dft_pair(size_count):
    index_row = jnp.arange(size_count, dtype=jnp.int32)
    phase = (index_row[:, None] * index_row[None, :] % size_count).astype(jnp.float32) * (
        -2.0 * math.pi / size_count
    )
    return (jnp.cos(phase), jnp.sin(phase))


def twist(spectrum, sign):
    outer_len = spectrum.shape[1]
    total = outer_len * inner_len
    outer_index = jnp.arange(outer_len, dtype=jnp.int32)[:, None, None]
    inner_index = jnp.arange(inner_len, dtype=jnp.int32)[None, None, :]
    phase = (outer_index * inner_index % total).astype(jnp.float32) * (-2.0 * math.pi / total)
    tw_real = jnp.cos(phase)
    tw_imag = jnp.sin(phase) * sign
    real_part = spectrum[0] * tw_real - spectrum[1] * tw_imag
    imag_part = spectrum[0] * tw_imag + spectrum[1] * tw_real
    return jnp.stack([real_part, imag_part])


def last_matrix(sign):
    last_real, last_imag = dft_pair(inner_len)
    last_imag = last_imag * sign
    return jnp.stack([jnp.stack([last_real, -last_imag]), jnp.stack([last_imag, last_real])])


def apply_last(spectrum, sign):
    return jnp.einsum(
        "qzcn,pqkn->pzck", spectrum, last_matrix(sign), precision=lax.Precision.HIGHEST
    )


def forward_spectrum(signal):
    half_rows = signal.shape[0]
    outer_len = 2 * half_rows
    lead_real, lead_imag = dft_pair(outer_len)
    lead = jnp.stack([lead_real[:, :half_rows], lead_imag[:, :half_rows]])
    spectrum = jnp.einsum("pzn,ncm->pzcm", lead, signal, precision=lax.Precision.HIGHEST)
    return apply_last(twist(spectrum, 1.0), 1.0)


def inverse_spectrum(spectrum, want_imag):
    outer_len = spectrum.shape[1]
    half_rows = outer_len // 2
    spectrum = twist(apply_last(spectrum, -1.0), -1.0)
    lead_real, lead_imag = dft_pair(outer_len)
    lead_real = lead_real[:half_rows]
    lead_imag = lead_imag[:half_rows]
    scale = 1.0 / (outer_len * inner_len)
    if want_imag:
        lead = jnp.stack([jnp.stack([lead_real, lead_imag]), jnp.stack([-lead_imag, lead_real])])
    else:
        lead = jnp.stack([lead_real, lead_imag])[None]
    return jnp.einsum("qzcm,pqtz->ptcm", spectrum, lead * scale, precision=lax.Precision.HIGHEST)


def to_blocks(array):
    seq_len, chans = array.shape
    return (
        array.astype(jnp.float32).reshape(seq_len // inner_len, inner_len, chans).transpose(0, 2, 1)
    )


def from_blocks(array):
    half_rows, chans, unused = array.shape
    return array.transpose(0, 2, 1).reshape(half_rows * inner_len, chans)


def channel_work(mixed, gated, filters):
    seq_len, chans = mixed.shape
    group_count = filters.shape[0]
    group_size = chans // group_count
    half_rows = seq_len // inner_len
    outer_len = 2 * half_rows
    split_shape = (2, outer_len, group_count, group_size, inner_len)
    mix_spec = forward_spectrum(to_blocks(mixed)).reshape(split_shape)
    gate_spec = forward_spectrum(to_blocks(gated)).reshape(split_shape)
    filter_blocks = filters.reshape(group_count, half_rows, inner_len).transpose(1, 0, 2)
    filt_spec = forward_spectrum(filter_blocks)[:, :, :, None, :]
    filt_real, filt_imag = (filt_spec[0], filt_spec[1])
    mix_real, mix_imag = (mix_spec[0], mix_spec[1])
    gate_real, gate_imag = (gate_spec[0], gate_spec[1])
    conv_real = filt_real * mix_real - filt_imag * mix_imag
    conv_imag = filt_real * mix_imag + filt_imag * mix_real
    corr_real = filt_real * gate_real + filt_imag * gate_imag
    corr_imag = filt_real * gate_imag - filt_imag * gate_real
    combined = jnp.stack([conv_real - corr_imag, conv_imag + corr_real]).reshape(
        2, outer_len, chans, inner_len
    )
    both = inverse_spectrum(combined, True)
    conv_out = from_blocks(both[0])
    mixed_grad = from_blocks(both[1])
    lag_real = jnp.sum(mix_real * gate_real + mix_imag * gate_imag, axis=2)
    lag_imag = jnp.sum(mix_real * gate_imag - mix_imag * gate_real, axis=2)
    lag_out = inverse_spectrum(jnp.stack([lag_real, lag_imag]), False)[0]
    filter_grad = lag_out.transpose(1, 0, 2).reshape(group_count, seq_len) * (
        group_size * seq_len
    ) ** (-0.5)
    return (conv_out, mixed_grad, filter_grad)


def rounded_product(left, right):
    product = (left.astype(jnp.float32) * right.astype(jnp.float32)).astype(jnp.bfloat16)
    return lax.optimization_barrier(product)


def per_device(query_proj, key_proj, value_proj, cotangent, out_weight, filters):
    grad_rows = jnp.einsum(
        "tj,cj->tc",
        cotangent,
        lax.all_gather(out_weight, "ctx", axis=0, tiled=True),
        preferred_element_type=jnp.float32,
    ).astype(jnp.bfloat16)
    query_cols, key_cols, value_cols, grad_cols = (
        lax.all_to_all(query_proj, "ctx", split_axis=1, concat_axis=0, tiled=True),
        lax.all_to_all(key_proj, "ctx", split_axis=1, concat_axis=0, tiled=True),
        lax.all_to_all(value_proj, "ctx", split_axis=1, concat_axis=0, tiled=True),
        lax.all_to_all(grad_rows, "ctx", split_axis=1, concat_axis=0, tiled=True),
    )
    mixed_cols = rounded_product(key_cols, value_cols)
    gated_cols = rounded_product(query_cols, grad_cols)
    conv_out, mixed_grad, filter_grad = channel_work(mixed_cols, gated_cols, filters)
    query_grad_cols = grad_cols.astype(jnp.float32) * conv_out
    query_grad, key_grad, value_grad = (
        lax.all_to_all(query_grad_cols, "ctx", split_axis=0, concat_axis=1, tiled=True),
        lax.all_to_all(
            mixed_grad * value_cols.astype(jnp.float32),
            "ctx",
            split_axis=0,
            concat_axis=1,
            tiled=True,
        ),
        lax.all_to_all(
            mixed_grad * key_cols.astype(jnp.float32),
            "ctx",
            split_axis=0,
            concat_axis=1,
            tiled=True,
        ),
    )
    return (query_grad, key_grad, value_grad, filter_grad)


def solution(mesh):
    placed = (
        P(("parts", "ctx"), None),
        P(("parts", "ctx"), None),
        P(("parts", "ctx"), None),
        P(("parts", "ctx"), None),
        P("ctx", None),
        P("ctx", None),
    )
    return jax.shard_map(
        per_device,
        mesh=mesh,
        in_specs=placed,
        out_specs=(
            P(("parts", "ctx"), None),
            P(("parts", "ctx"), None),
            P(("parts", "ctx"), None),
            P(("parts", "ctx"), None),
        ),
        check_vma=False,
    )
```

profile of v0, /device:TPU:12, one launch (start us, length us, event | category | flops | bytes accessed | tf_op | source)
XLA Modules:
  0.0 509.2 jit_solution(12436188474592288112)
XLA Ops:
  7.9 2.3 copy.98
  10.2 6.4 %all-to-all-start.1 = ((bf16[128,16,256]{0,2,1:T(8,128)(2,1)}), bf16[128,16,256]{0,2,1:T(8,128)(2,1)S(1)}, u32[]{:S(2)}, u32[]{:S(2)}) async-start(bf16[128,16,256]{0,2,1:T(8,128)(2,1)} %bitcast.30), calls=%async_computation.1 | async-start | bytes 2097152 | tf_op jit(solution)/shard_map/all_to_all | solution.py:127
  16.6 1.3 copy.100
  17.9 47.6 %all-to-all-done.1 = bf16[128,16,256]{0,2,1:T(8,128)(2,1)S(1)} async-done(((bf16[128,16,256]{0,2,1:T(8,128)(2,1)}), bf16[128,16,256]{0,2,1:T(8,128)(2,1)S(1)}, u32[]{:S(2)}, u32[]{:S(2)}) %all-to-all-start.1) | async-done | bytes 1048608 | tf_op jit(solution)/shard_map/all_to_all | solution.py:127
  65.5 6.1 %all-to-all-start.2 = ((bf16[128,16,256]{0,2,1:T(8,128)(2,1)}), bf16[128,16,256]{0,2,1:T(8,128)(2,1)S(1)}, u32[]{:S(2)}, u32[]{:S(2)}) async-start(bf16[128,16,256]{0,2,1:T(8,128)(2,1)} %bitcast.224), calls=%async_computation.2 | async-start | bytes 2097152 | tf_op jit(solution)/shard_map/all_to_all | solution.py:128
  71.6 2.3 copy.107
  73.9 45.8 %all-to-all-done.2 = bf16[128,16,256]{0,2,1:T(8,128)(2,1)S(1)} async-done(((bf16[128,16,256]{0,2,1:T(8,128)(2,1)}), bf16[128,16,256]{0,2,1:T(8,128)(2,1)S(1)}, u32[]{:S(2)}, u32[]{:S(2)}) %all-to-all-start.2) | async-done | bytes 1048608 | tf_op jit(solution)/shard_map/all_to_all | solution.py:128
  119.7 7.3 %all-to-all-start.3 = ((bf16[128,16,256]{0,2,1:T(8,128)(2,1)}), bf16[128,16,256]{0,2,1:T(8,128)(2,1)}, u32[]{:S(2)}, u32[]{:S(2)}) async-start(bf16[128,16,256]{0,2,1:T(8,128)(2,1)} %bitcast.223), calls=%async_computation.3 | async-start | bytes 2097152 | tf_op jit(solution)/shard_map/all_to_all | solution.py:126
  128.8 57.3 %all-gather.2.cloned.1.call-done = bf16[4096,2048]{1,0:T(8,128)(2,1)} async-done(((bf16[256,2048]{1,0:T(8,128)(2,1)}), bf16[4096,2048]{1,0:T(8,128)(2,1)}) %all-gather.2.cloned.1.call-update) | async-done | bytes 16777232 | tf_op jit(solution)/shard_map/all_gather | solution.py:122
  186.2 12.4 %convolution_convert_fusion = bf16[128,4096]{1,0:T(8,128)(2,1)} fusion(bf16[128,2048]{1,0:T(8,128)(2,1)S(1)} %copy-done, bf16[4096,2048]{1,0:T(8,128)(2,1)} %all-gather.2.cloned.1.call-done), kind=kOutput, calls=%fused_computation.13 | convolution fusion | flops 2148007936 | bytes 18350080 | tf_op jit(solution)/shard_map/tj,cj->tc/dot_general | solution.py:119
  198.5 2.3 copy.145
  200.8 10.3 %all-to-all-start = ((bf16[128,16,256]{0,2,1:T(8,128)(2,1)}), bf16[128,16,256]{0,2,1:T(8,128)(2,1)}, u32[]{:S(2)}, u32[]{:S(2)}) async-start(bf16[128,16,256]{0,2,1:T(8,128)(2,1)} %bitcast.222), calls=%async_computation | async-start | bytes 2097152 | tf_op jit(solution)/shard_map/all_to_all | solution.py:129
  212.6 2.3 mul.851
  214.9 5.7 %copy.104 = f32[1,32,256,128]{2,3,1,0:T(8,128)} copy(f32[1,32,256,128]{3,2,1,0:T(8,128)} %bitcast.214) | data formatting | bytes 8388608 | tf_op jit(solution)/shard_map/mul | solution.py:94
  220.7 2.3 mul.862
  223.0 5.6 %copy.106 = f32[1,32,256,128]{2,3,1,0:T(8,128)} copy(f32[1,32,256,128]{3,2,1,0:T(8,128)} %bitcast.215) | data formatting | bytes 8388608 | tf_op jit(solution)/shard_map/mul | solution.py:94
  228.8 1.2 fusion.19
  230.5 5.6 %fusion.26 = f32[2,32,256,128]{3,1,2,0:T(8,128)} fusion(bf16[16,128,256]{1,0,2:T(8,128)(2,1)S(1)} %bitcast.218, f32[1,32,16]{2,1,0:T(8,128)S(1)} %get-tuple-element.47, f32[1,32,16]{2,1,0:T(8,128)S(1)} %get-tuple-element.48), kind=kOutput, calls=%fused_computation.48 | convolution fusion | flops 402654208 | bytes 9441280 | tf_op jit(solution)/shard_map/pzn,ncm->pzcm/dot_general | solution.py:49
  236.1 2.8 fusion.22
  239.4 3.4 fusion.24
  242.8 6.2 %multiply_subtract_fusion.3 = (f32[1,32,256,128]{3,1,2,0:T(8,128)}, f32[1,32,256,128]{3,1,2,0:T(8,128)}, f32[1,32,256,128]{3,1,2,0:T(8,128)S(1)}, f32[1,32,256,128]{3,1,2,0:T(8,128)}) fusion(f32[2,32,256,128]{3,1,2,0:T(8,128)S(1)} %bitcast.212, f32[32,128]{1,0:T(8,128)S(1)} %get-tuple-element.49, f32[32,128]{1,0:T(8,128)S(1)} %get-tuple-element.50, ...), kind=kLoop, calls=%fused_computation.23 | loop fusion | flops 12582912 | bytes 33587200 | tf_op jit(solution)/shard_map/sub | solution.py:27
  249.1 4.5 pad_maximum_fusion
  253.6 12.6 %fusion.9 = f32[2,32,256,128]{2,3,1,0:T(8,128)S(1)} fusion(f32[2,32,256,128]{3,1,2,0:T(8,128)S(1)} %pad_maximum_fusion, f32[1,2,128,128]{3,2,1,0:T(8,128)S(1)} %copy-done.6, f32[1,2,128,128]{3,2,1,0:T(8,128)S(1)} %copy-done.8), kind=kOutput, calls=%fused_computation.24 | convolution fusion | flops 6442516480 | bytes 17039360 | tf_op jit(solution)/shard_map/qzcn,pqkn->pzck/dot_general | solution.py:39
  266.2 3.2 pad_maximum_fusion.1
  269.4 16.7 %fusion.12 = f32[2,32,256,128]{2,3,1,0:T(8,128)} fusion(f32[2,32,256,128]{3,1,2,0:T(8,128)S(1)} %pad_maximum_fusion.1, f32[1,2,128,128]{3,2,1,0:T(8,128)S(1)} %copy-done.6, f32[1,2,128,128]{3,2,1,0:T(8,128)S(1)} %copy-done.8), kind=kOutput, calls=%fused_computation.25 | convolution fusion | flops 6442516480 | bytes 17039360 | tf_op jit(solution)/shard_map/qzcn,pqkn->pzck/dot_general | solution.py:39
  286.1 10.2 %multiply_add_fusion = (f32[1,32,256,128]{2,3,1,0:T(8,128)}, f32[1,32,256,128]{2,3,1,0:T(8,128)}, f32[1,32,256,128]{2,3,1,0:T(8,128)}, f32[1,32,256,128]{2,3,1,0:T(8,128)}) fusion(f32[2,32,256,128]{2,3,1,0:T(8,128)} %fusion.12, f32[2,32,256,128]{2,3,1,0:T(8,128)S(1)} %fusion.9, f32[1,32,256,128]{2,3,1,0:T(8,128)} %copy.106, f32[1,32,256,128]{2,3,1,0:T(8,128)S(1)} %copy-done.2), kind=kLoop, calls=%fused_computation.15 | loop fusion | flops 20971520 | bytes 41943040 | tf_op jit(solution)/shard_map/add | solution.py:104
  296.4 7.8 %maximum_bitcast_fusion = f32[2,32,256,128,1]{2,3,1,0,4:T(8,128)} fusion(f32[1,32,256,128]{2,3,1,0:T(8,128)} %get-tuple-element.20, f32[1,32,256,128]{2,3,1,0:T(8,128)} %get-tuple-element.21), kind=kLoop, calls=%fused_computation.2 | loop fusion | flops 2097152 | bytes 16777216 | tf_op jit(solution)/shard_map/stack | solution.py:98
  304.1 10.3 %copy.139 = f32[2,32,256,128,1]{3,1,0,2,4:T(8,128)} copy(f32[2,32,256,128,1]{2,3,1,0,4:T(8,128)} %maximum_bitcast_fusion) | data formatting | bytes 16777216 | tf_op jit(solution)/shard_map/stack | solution.py:98
  314.4 12.5 %convolution_bitcast_fusion = f32[2,32,256,128]{3,1,2,0:T(8,128)S(1)} fusion(f32[2,32,256,128,1]{3,1,0,2,4:T(8,128)} %copy.139, f32[1,2,128,128]{3,2,1,0:T(8,128)S(1)} %copy-done.11, f32[1,2,128,128]{3,2,1,0:T(8,128)S(1)} %copy-done.9), kind=kOutput, calls=%fused_computation.26 | convolution fusion | flops 6442516480 | bytes 17039360 | tf_op jit(solution)/shard_map/qzcn,pqkn->pzck/dot_general | solution.py:39
  326.9 1.3 multiply_subtract_fusion.1
  328.3 5.0 fusion.15
  333.3 5.3 %fusion.18 = (f32[16,128,256]{1,0,2:T(8,128)}, f32[16,128,256]{1,0,2:T(8,128)}, f32[16,128,256]{1,0,2:T(8,128)S(1)}) fusion(f32[2,16,256,128]{3,1,2,0:T(8,128)S(1)} %fusion.15, bf16[128,16,256]{0,2,1:T(8,128)(2,1)S(1)} %all-to-all-done.1, bf16[128,16,256]{0,2,1:T(8,128)(2,1)S(1)} %copy-done.4, bf16[128,16,256]{0,2,1:T(8,128)(2,1)} %all-to-all-done), kind=kLoop, calls=%fused_computation.33 | loop fusion | flops 3145728 | bytes 13631488 | tf_op jit(solution)/shard_map/mul | solution.py:145
  338.6 2.0 copy.120
  340.6 6.1 %all-to-all-start.4 = ((f32[16,128,256]{1,2,0:T(8,128)}), f32[16,128,256]{1,2,0:T(8,128)S(1)}, u32[]{:S(2)}, u32[]{:S(2)}) async-start(f32[16,128,256]{1,2,0:T(8,128)} %copy.120), calls=%async_computation.4 | async-start | bytes 4194304 | tf_op jit(solution)/shard_map/all_to_all | solution.py:136
  346.7 3.6 copy.121
  350.3 43.7 %all-to-all-done.4 = f32[16,128,256]{1,2,0:T(8,128)S(1)} async-done(((f32[16,128,256]{1,2,0:T(8,128)}), f32[16,128,256]{1,2,0:T(8,128)S(1)}, u32[]{:S(2)}, u32[]{:S(2)}) %all-to-all-start.4) | async-done | bytes 2097184 | tf_op jit(solution)/shard_map/all_to_all | solution.py:136
  393.9 5.1 all-to-all-start.5
  399.0 3.7 copy.122
  402.6 43.7 %all-to-all-done.5 = f32[16,128,256]{1,2,0:T(8,128)} async-done(((f32[16,128,256]{1,2,0:T(8,128)}), f32[16,128,256]{1,2,0:T(8,128)}, u32[]{:S(2)}, u32[]{:S(2)}) %all-to-all-start.5) | async-done | bytes 2097184 | tf_op jit(solution)/shard_map/all_to_all | solution.py:137
  446.4 5.5 %all-to-all-start.6 = ((f32[16,128,256]{1,2,0:T(8,128)}), f32[16,128,256]{1,2,0:T(8,128)}, u32[]{:S(2)}, u32[]{:S(2)}) async-start(f32[16,128,256]{1,2,0:T(8,128)} %copy.122), calls=%async_computation.6 | async-start | bytes 4194304 | tf_op jit(solution)/shard_map/all_to_all | solution.py:144
  451.8 5.6 %copy.125 = f32[1,32,256,128]{3,2,1,0:T(8,128)} copy(f32[1,32,256,128]{2,3,1,0:T(8,128)} %get-tuple-element.19) | data formatting | bytes 8388608 | tf_op jit(solution)/shard_map/sub | solution.py:105
  457.4 2.9 reduce_sum.19
  460.4 5.6 %copy.123 = f32[1,32,256,128]{3,2,1,0:T(8,128)} copy(f32[1,32,256,128]{2,3,1,0:T(8,128)} %get-tuple-element.18) | data formatting | bytes 8388608 | tf_op jit(solution)/shard_map/add | solution.py:104
  466.0 2.9 reduce_sum.18
  470.8 1.8 copy.128
  472.6 2.9 copy.129
  475.6 23.4 %all-to-all-done.6 = f32[16,128,256]{1,2,0:T(8,128)} async-done(((f32[16,128,256]{1,2,0:T(8,128)}), f32[16,128,256]{1,2,0:T(8,128)}, u32[]{:S(2)}, u32[]{:S(2)}) %all-to-all-start.6) | async-done | bytes 2097184 | tf_op jit(solution)/shard_map/all_to_all | solution.py:144
  499.0 2.9 copy.130
  (75 shorter events, 7.3 us)
Async XLA Ops:
  7.2 179.0 %copy-start = (bf16[128,2048]{1,0:T(8,128)(2,1)S(1)}, bf16[128,2048]{1,0:T(8,128)(2,1)}, u32[]{:S(2)}) copy-start(bf16[128,2048]{1,0:T(8,128)(2,1)} %param.9) | copy-start | bytes 1572868
  7.2 9.4 %copy-start.13 = (bf16[128,4096]{1,0:T(8,128)(2,1)S(1)}, bf16[128,4096]{1,0:T(8,128)(2,1)}, u32[]{:S(2)}) copy-start(bf16[128,4096]{1,0:T(8,128)(2,1)} %param.8) | copy-start | bytes 3145732
  7.2 179.0 %all-gather.2.cloned.1.call-start = ((), (), s32[]{:S(2)}) async-start(), calls=%async_computation.7 | async-start | bytes 17825792 | tf_op jit(solution)/shard_map/all_gather | solution.py:122
  10.2 63.7 %copy-start.14 = (f32[16,2048]{1,0:T(8,128)S(1)}, f32[16,2048]{1,0:T(8,128)}, u32[]{:S(2)}) copy-start(f32[16,2048]{1,0:T(8,128)} %param.11) | copy-start | bytes 393220
  10.2 55.3 %all-to-all-start.1 = ((bf16[128,16,256]{0,2,1:T(8,128)(2,1)}), bf16[128,16,256]{0,2,1:T(8,128)(2,1)S(1)}, u32[]{:S(2)}, u32[]{:S(2)}) async-start(bf16[128,16,256]{0,2,1:T(8,128)(2,1)} %bitcast.30), calls=%async_computation.1 | async-start | bytes 2097152 | tf_op jit(solution)/shard_map/all_to_all | solution.py:127
  65.5 54.2 %all-to-all-start.2 = ((bf16[128,16,256]{0,2,1:T(8,128)(2,1)}), bf16[128,16,256]{0,2,1:T(8,128)(2,1)S(1)}, u32[]{:S(2)}, u32[]{:S(2)}) async-start(bf16[128,16,256]{0,2,1:T(8,128)(2,1)} %bitcast.224), calls=%async_computation.2 | async-start | bytes 2097152 | tf_op jit(solution)/shard_map/all_to_all | solution.py:128
  119.7 109.1 %copy-start.3 = (bf16[128,16,256]{0,2,1:T(8,128)(2,1)}, bf16[128,16,256]{0,2,1:T(8,128)(2,1)S(1)}, u32[]{:S(2)}) copy-start(bf16[128,16,256]{0,2,1:T(8,128)(2,1)S(1)} %all-to-all-done.2) | copy-start | bytes 3145732
  119.7 81.1 %all-to-all-start.3 = ((bf16[128,16,256]{0,2,1:T(8,128)(2,1)}), bf16[128,16,256]{0,2,1:T(8,128)(2,1)}, u32[]{:S(2)}, u32[]{:S(2)}) async-start(bf16[128,16,256]{0,2,1:T(8,128)(2,1)} %bitcast.223), calls=%async_computation.3 | async-start | bytes 2097152 | tf_op jit(solution)/shard_map/all_to_all | solution.py:126
  128.8 82.9 %copy-start.5 = (f32[1,2,128,128]{3,2,1,0:T(8,128)}, f32[1,2,128,128]{3,2,1,0:T(8,128)S(1)}, u32[]{:S(2)}) copy-start(f32[1,2,128,128]{3,2,1,0:T(8,128)S(1)} %get-tuple-element.38) | copy-start | bytes 393220
  128.8 82.9 %copy-start.7 = (f32[1,2,128,128]{3,2,1,0:T(8,128)}, f32[1,2,128,128]{3,2,1,0:T(8,128)S(1)}, u32[]{:S(2)}) copy-start(f32[1,2,128,128]{3,2,1,0:T(8,128)S(1)} %get-tuple-element.39) | copy-start | bytes 393220
  200.8 35.3 %all-to-all-start = ((bf16[128,16,256]{0,2,1:T(8,128)(2,1)}), bf16[128,16,256]{0,2,1:T(8,128)(2,1)}, u32[]{:S(2)}, u32[]{:S(2)}) async-start(bf16[128,16,256]{0,2,1:T(8,128)(2,1)} %bitcast.222), calls=%async_computation | async-start | bytes 2097152 | tf_op jit(solution)/shard_map/all_to_all | solution.py:129
  228.7 7.4 %copy-start.15 = (f32[1,16,32]{2,1,0:T(8,128)}, f32[1,16,32]{2,1,0:T(8,128)S(1)}, u32[]{:S(2)}) copy-start(f32[1,16,32]{2,1,0:T(8,128)S(1)} %get-tuple-element.43) | copy-start | bytes 6148
  228.7 7.4 %copy-start.17 = (f32[1,16,32]{2,1,0:T(8,128)}, f32[1,16,32]{2,1,0:T(8,128)S(1)}, u32[]{:S(2)}) copy-start(f32[1,16,32]{2,1,0:T(8,128)S(1)} %get-tuple-element.55) | copy-start | bytes 6148
  239.2 3.6 slice-start
  239.4 3.4 slice-start.1
  249.0 4.5 copy-start.6
  249.1 4.5 copy-start.8
  269.4 16.7 %copy-start.2 = (f32[1,32,256,128]{2,3,1,0:T(8,128)S(1)}, f32[1,32,256,128]{2,3,1,0:T(8,128)}, u32[]{:S(2)}) copy-start(f32[1,32,256,128]{2,3,1,0:T(8,128)} %copy.104) | copy-start | bytes 12582916
  304.1 10.3 %copy-start.9 = (f32[1,2,128,128]{3,2,1,0:T(8,128)S(1)}, f32[1,2,128,128]{3,2,1,0:T(8,128)}, u32[]{:S(2)}) copy-start(f32[1,2,128,128]{3,2,1,0:T(8,128)} %get-tuple-element.37) | copy-start | bytes 393220
  304.1 10.3 %copy-start.11 = (f32[1,2,128,128]{3,2,1,0:T(8,128)S(1)}, f32[1,2,128,128]{3,2,1,0:T(8,128)}, u32[]{:S(2)}) copy-start(f32[1,2,128,128]{3,2,1,0:T(8,128)} %get-tuple-element.40) | copy-start | bytes 393220
  328.3 5.0 copy-start.4
  340.6 53.3 %all-to-all-start.4 = ((f32[16,128,256]{1,2,0:T(8,128)}), f32[16,128,256]{1,2,0:T(8,128)S(1)}, u32[]{:S(2)}, u32[]{:S(2)}) async-start(f32[16,128,256]{1,2,0:T(8,128)} %copy.120), calls=%async_computation.4 | async-start | bytes 4194304 | tf_op jit(solution)/shard_map/all_to_all | solution.py:136
  393.9 52.4 %all-to-all-start.5 = ((f32[16,128,256]{1,2,0:T(8,128)}), f32[16,128,256]{1,2,0:T(8,128)}, u32[]{:S(2)}, u32[]{:S(2)}) async-start(f32[16,128,256]{1,2,0:T(8,128)} %copy.121), calls=%async_computation.5 | async-start | bytes 4194304 | tf_op jit(solution)/shard_map/all_to_all | solution.py:137
  446.4 52.7 %all-to-all-start.6 = ((f32[16,128,256]{1,2,0:T(8,128)}), f32[16,128,256]{1,2,0:T(8,128)}, u32[]{:S(2)}, u32[]{:S(2)}) async-start(f32[16,128,256]{1,2,0:T(8,128)} %copy.122), calls=%async_computation.6 | async-start | bytes 4194304 | tf_op jit(solution)/shard_map/all_to_all | solution.py:144
  466.0 3.0 copy-start.10
  466.0 3.0 copy-start.12
  466.0 3.8 copy-start.16
  466.0 3.8 copy-start.18
  472.6 29.3 %copy-start.1 = (bf16[128,2048]{1,0:T(8,128)(2,1)S(1)}, bf16[128,2048]{1,0:T(8,128)(2,1)}, u32[]{:S(2)}) copy-start(bf16[128,2048]{1,0:T(8,128)(2,1)} %param.9) | copy-start | bytes 1572868
Sparse Core Ops, SparseCore 0:
  10.2 175.9 all-gather.1
where the time goes:
time: 516 us; the launch traced here: 509 us
  waiting for transfers between devices  262 us (51%)
  matrix products  70.3 us (14%)
  local copies, waits for them, and re-layouts  64.6 us (13%)
  other arithmetic  50.4 us (10%)
  starting transfers between devices  46.7 us (9%)
  between operations  14.9 us (3%)
    all_gather x1, waiting for transfers between devices, per_device(): lax.all_gather(out_weight, 'ctx', axis=0, tiled=True)  57.3 us
    all_to_all x1, waiting for transfers between devices, per_device(): lax.all_to_all(key_proj, 'ctx', split_axis=1, concat_axis=0, tiled=True)  47.6 us
    all_to_all x1, waiting for transfers between devices, per_device(): lax.all_to_all(value_proj, 'ctx', split_axis=1, concat_axis=0, tiled=True)  45.8 us
    all_to_all x1, waiting for transfers between devices, per_device(): lax.all_to_all(mixed_grad * value_cols.astype(jnp.float32), 'ctx', split_...  43.7 us
    all_to_all x1, waiting for transfers between devices, per_device(): lax.all_to_all(query_grad_cols, 'ctx', split_axis=0, concat_axis=1, tiled...  43.7 us
    dot_general x5, matrix products, apply_last(): jnp.einsum('qzcn,pqkn->pzck', spectrum, last_matrix(sign), precision=lax....  43 us
    all_to_all x1, waiting for transfers between devices, per_device(): lax.all_to_all(mixed_grad * key_cols.astype(jnp.float32), 'ctx', split_ax...  23.4 us
    mul x7, local copies, waits for them, and re-layouts, channel_work(): conv_real = filt_real * mix_real - filt_imag * mix_imag  16.2 us
  transfers between devices with their start and end apart: 8, of which 6 were waited for; matrix products, arithmetic and copies ran while one was open for 15% of the time, Pallas kernels for 0%

commit v1 on v0

--- a/solution.py
+++ b/solution.py
@@ -3,6 +3,9 @@
 import jax
 import jax.numpy as jnp
 from jax import lax
+from jax.experimental import pallas as pl
+from jax.experimental.pallas import tpu as pltpu
+from jax.sharding import Mesh
 from jax.sharding import PartitionSpec as P
 
 inner_len = 128
@@ -115,7 +118,7 @@
     return lax.optimization_barrier(product)
 
 
-def per_device(query_proj, key_proj, value_proj, cotangent, out_weight, filters):
+def per_device_spectral(query_proj, key_proj, value_proj, cotangent, out_weight, filters):
     grad_rows = jnp.einsum(
         "tj,cj->tc",
         cotangent,
@@ -152,24 +155,423 @@
     return (query_grad, key_grad, value_grad, filter_grad)
 
 
+line_len = 4
+quad_len = 4
+lane = 128
+group_width = 16
+
+
+def nt_dot(left, right):
+    return lax.dot_general(left, right, (((1,), (1,)), ((), ())), preferred_element_type=jnp.float32)
+
+
+def split_kernel(*refs):
+    count = (len(refs) - 1) // line_len - 1
+    outs = refs[-line_len:]
+    for step in range(line_len):
+        block = refs[1 + count * step][...].astype(jnp.float32)
+        if count == 2:
+            block = block * refs[2 + count * step][...].astype(jnp.float32)
+        outs[step][...] = block.T.astype(jnp.bfloat16)
+
+
+def split_columns(place, *arrays):
+    rows, chans = arrays[0].shape
+    piece = chans // line_len
+    cut = 2
+    in_specs = []
+    for step in range(line_len):
+        for _ in arrays:
+            in_specs.append(
+                pl.BlockSpec(
+                    (rows, piece // cut), lambda i, z, step=step: (0, (z[0] ^ step) * cut + i)
+                )
+            )
+    return pl.pallas_call(
+        split_kernel,
+        grid_spec=pltpu.PrefetchScalarGridSpec(
+            num_scalar_prefetch=1,
+            grid=(cut,),
+            in_specs=in_specs,
+            out_specs=[pl.BlockSpec((piece // cut, rows), lambda i, z: (i, 0))] * line_len,
+        ),
+        out_shape=[jax.ShapeDtypeStruct((piece, rows), jnp.bfloat16)] * line_len,
+        name="split_columns",
+    )(place, *(list(arrays) * line_len))
+
+
+def toeplitz_kernel(filter_ref, conv_ref, corr_ref):
+    seq_len = filter_ref.shape[-1]
+    wide = jnp.broadcast_to(filter_ref[0], (lane, seq_len))
+    strip = pltpu.roll(wide, 0, 1, stride=1, stride_axis=0)
+    row = lax.broadcasted_iota(jnp.int32, (lane, lane), 0)
+    col = lax.broadcasted_iota(jnp.int32, (lane, lane), 1)
+    for lag in range(seq_len // lane):
+        tile = strip[:, lag * lane : (lag + 1) * lane]
+        if lag == 0:
+            tile = jnp.where(col >= row, tile, 0.0)
+        rows = slice((lag % 2) * lane, (lag % 2 + 1) * lane)
+        cols = slice((lag // 2) * lane, (lag // 2 + 1) * lane)
+        conv_ref[0, rows, cols] = tile.astype(jnp.bfloat16)
+        corr_ref[0, rows, cols] = tile.T.astype(jnp.bfloat16)
+
+
+def toeplitz_tiles(filters):
+    groups, seq_len = filters.shape
+    shape = jax.ShapeDtypeStruct((groups, 2 * lane, seq_len // 2), jnp.bfloat16)
+    spec = pl.BlockSpec((1, 2 * lane, seq_len // 2), lambda g: (g, 0, 0))
+    return pl.pallas_call(
+        toeplitz_kernel,
+        grid=(groups,),
+        in_specs=[pl.BlockSpec((1, 1, seq_len), lambda g: (g, 0, 0))],
+        out_specs=[spec, spec],
+        out_shape=[shape, shape],
+        name="toeplitz_tiles",
+    )(filters.reshape(groups, 1, seq_len))
+
+
+def conv_kernel(place_ref, *refs):
+    signals = refs[:line_len]
+    tile_ref, out_ref = refs[line_len:]
+    rows = line_len * quad_len * group_width
+    signal = jnp.concatenate([s[...].reshape(quad_len * group_width, lane) for s in signals], axis=0)
+    late = jnp.concatenate(
+        [jnp.zeros((group_width, lane), signal.dtype), signal[: rows - group_width]], axis=0
+    )
+    both = jnp.concatenate([signal, late], axis=1)
+    total = jnp.zeros((rows, lane), jnp.float32)
+    for pair in range(0, line_len * quad_len // 2, 2):
+        skip = 2 * group_width * pair
+        part = jnp.dot(
+            both[: rows - skip],
+            tile_ref[0, :, pair * lane : (pair + 2) * lane],
+            preferred_element_type=jnp.float32,
+        )
+        near = total[skip:] + part[:, :lane]
+        shift = 2 * group_width
+        near = jnp.concatenate(
+            [near[:shift], near[shift:] + part[: rows - skip - shift, lane:]], axis=0
+        )
+        total = near if skip == 0 else jnp.concatenate([total[:skip], near], axis=0)
+    result = total.astype(jnp.bfloat16).reshape(line_len, quad_len, group_width, lane)
+    for z in range(line_len):
+        out_ref[:, z] = result[z]
+
+
+def convolve(place, mixed, tiles):
+    chans = mixed.shape[2]
+    groups = tiles.shape[0]
+    specs = [
+        pl.BlockSpec(
+            (quad_len, None, group_width, lane), lambda g, p, z=z: (0, p[0] ^ z, g, 0)
+        )
+        for z in range(line_len)
+    ]
+    return pl.pallas_call(
+        conv_kernel,
+        grid_spec=pltpu.PrefetchScalarGridSpec(
+            num_scalar_prefetch=1,
+            grid=(groups,),
+            in_specs=specs + [pl.BlockSpec((1,) + tiles.shape[1:], lambda g, p: (g, 0, 0))],
+            out_specs=pl.BlockSpec(
+                (quad_len, line_len, group_width, lane), lambda g, p: (0, 0, g, 0)
+            ),
+        ),
+        out_shape=jax.ShapeDtypeStruct((quad_len, line_len, chans, lane), jnp.bfloat16),
+        name="convolve",
+    )(place, *([mixed] * line_len), tiles)
+
+
+def corr_kernel(gated_ref, tile_ref, out_ref):
+    rows = line_len * quad_len * group_width
+    gated = jnp.concatenate(
+        [gated_ref[:, z].reshape(quad_len * group_width, lane) for z in range(line_len)], axis=0
+    )
+    early = jnp.concatenate(
+        [gated[group_width:], jnp.zeros((group_width, lane), gated.dtype)], axis=0
+    )
+    both = jnp.concatenate([gated, early], axis=1)
+    total = jnp.zeros((rows, lane), jnp.float32)
+    shift = 2 * group_width
+    for pair in range(0, line_len * quad_len // 2, 2):
+        skip = shift * pair
+        part = jnp.dot(
+            both[skip:],
+            tile_ref[0, :, pair * lane : (pair + 2) * lane],
+            preferred_element_type=jnp.float32,
+        )
+        near = total[: rows - skip] + part[:, :lane]
+        near = jnp.concatenate(
+            [near[: rows - skip - shift] + part[shift:, lane:], near[rows - skip - shift :]], axis=0
+        )
+        total = near if skip == 0 else jnp.concatenate([near, total[rows - skip :]], axis=0)
+    result = total.astype(jnp.bfloat16).reshape(line_len, quad_len, group_width, lane)
+    for z in range(line_len):
+        out_ref[:, z] = result[z]
+
+
+def correlate(gated, tiles):
+    groups = tiles.shape[0]
+    spec = pl.BlockSpec((quad_len, line_len, group_width, lane), lambda g: (0, 0, g, 0))
+    return pl.pallas_call(
+        corr_kernel,
+        grid=(groups,),
+        in_specs=[spec, pl.BlockSpec((1,) + tiles.shape[1:], lambda g: (g, 0, 0))],
+        out_specs=spec,
+        out_shape=jax.ShapeDtypeStruct(gated.shape, jnp.bfloat16),
+        name="correlate",
+    )(gated, tiles)
+
+
+def lag_kernel(place_ref, *refs):
+    signals = refs[:line_len]
+    gated_ref, out_ref = refs[line_len:]
+    rows = line_len * quad_len * group_width
+    seq_len = line_len * quad_len * lane
+    mixed = jnp.concatenate([s[...].reshape(quad_len * group_width, lane) for s in signals], axis=0)
+    gated = jnp.concatenate(
+        [gated_ref[:, z].reshape(quad_len * group_width, lane) for z in range(line_len)]
+        + [jnp.zeros((rows, lane), gated_ref.dtype)],
+        axis=0,
+    )
+    flipped = mixed.astype(jnp.float32).T.astype(jnp.bfloat16)
+    parts = []
+    for lag in range(0, line_len * quad_len, 2):
+        first = gated[lag * group_width : lag * group_width + rows]
+        second = gated[(lag + 1) * group_width : (lag + 1) * group_width + rows]
+        parts.append(
+            jnp.dot(
+                flipped,
+                jnp.concatenate([first, second], axis=1),
+                preferred_element_type=jnp.float32,
+            )
+        )
+    row = lax.broadcasted_iota(jnp.int32, (lane, 2 * lane), 0)
+    col = lax.broadcasted_iota(jnp.int32, (lane, 2 * lane), 1)
+    parts[0] = jnp.where(col >= row, parts[0], 0.0)
+    total = jnp.concatenate(parts, axis=1)
+    half = lane // 2
+    while half >= 1:
+        total = total[:half] + pltpu.roll(total[half:], seq_len - half, 1)
+        half //= 2
+    out_ref[0] = total * (group_width * seq_len) ** (-0.5)
+
+
+def lag_sums(place, mixed, gated):
+    groups = gated.shape[2] // group_width
+    seq_len = line_len * quad_len * lane
+    specs = [
+        pl.BlockSpec(
+            (quad_len, None, group_width, lane), lambda g, p, z=z: (0, p[0] ^ z, g, 0)
+        )
+        for z in range(line_len)
+    ]
+    sums = pl.pallas_call(
+        lag_kernel,
+        grid_spec=pltpu.PrefetchScalarGridSpec(
+            num_scalar_prefetch=1,
+            grid=(groups,),
+            in_specs=specs
+            + [pl.BlockSpec((quad_len, line_len, group_width, lane), lambda g, p: (0, 0, g, 0))],
+            out_specs=pl.BlockSpec((1, 1, seq_len), lambda g, p: (g, 0, 0)),
+        ),
+        out_shape=jax.ShapeDtypeStruct((groups, 1, seq_len), jnp.float32),
+        name="lag_sums",
+    )(place, *([mixed] * line_len), gated)
+    return sums.reshape(groups, seq_len)
+
+
+def gate_kernel(place_ref, weight_ref, *refs):
+    cots = refs[:line_len]
+    queries = refs[line_len : 2 * line_len]
+    grad_ref, gated_ref = refs[2 * line_len :]
+    for step in range(line_len):
+        at = place_ref[0] ^ step
+        grad = nt_dot(weight_ref[...], cots[step][...]).astype(jnp.bfloat16)
+        grad_ref[0, at] = grad
+        query = queries[step][...].astype(jnp.float32)
+        gated_ref[0, at] = (query * grad.astype(jnp.float32)).astype(jnp.bfloat16)
+
+
+def gate(place, weights, cots, queries):
+    chans = weights.shape[0] // quad_len
+    feats = weights.shape[1]
+    near = line_len - 1
+    cot_specs = [
+        pl.BlockSpec(
+            (None, lane, feats), lambda i, z, k=k: (near + (z[0] ^ k) - z[0], 0, 0)
+        )
+        for k in range(line_len)
+    ]
+    spec = pl.BlockSpec((1, line_len, chans, lane), lambda i, z: (i, 0, 0, 0))
+    shape = jax.ShapeDtypeStruct((quad_len, line_len, chans, lane), jnp.bfloat16)
+    return pl.pallas_call(
+        gate_kernel,
+        grid_spec=pltpu.PrefetchScalarGridSpec(
+            num_scalar_prefetch=1,
+            grid=(quad_len,),
+            in_specs=[pl.BlockSpec((chans, feats), lambda i, z: (i, 0))]
+            + cot_specs
+            + [pl.BlockSpec((chans, lane), lambda i, z: (i, 0))] * line_len,
+            out_specs=[spec, spec],
+        ),
+        out_shape=[shape, shape],
+        name="gate",
+    )(place, weights, *([cots] * line_len), *queries)
+
+
+def query_kernel(place_ref, grad_ref, conv_ref, *outs):
+    for step in range(line_len):
+        at = place_ref[0] ^ step
+        product = grad_ref[0, at].astype(jnp.float32) * conv_ref[0, at].astype(jnp.float32)
+        outs[step][...] = product.astype(jnp.bfloat16)
+
+
+def query_pieces(place, grad, conv):
+    chans = grad.shape[2]
+    spec = pl.BlockSpec((1, line_len, chans, lane), lambda i, z: (i, 0, 0, 0))
+    return pl.pallas_call(
+        query_kernel,
+        grid_spec=pltpu.PrefetchScalarGridSpec(
+            num_scalar_prefetch=1,
+            grid=(quad_len,),
+            in_specs=[spec, spec],
+            out_specs=[pl.BlockSpec((chans, lane), lambda i, z: (i, 0))] * line_len,
+        ),
+        out_shape=[jax.ShapeDtypeStruct((quad_len * chans, lane), jnp.bfloat16)] * line_len,
+        name="query_pieces",
+    )(place, grad, conv)
+
+
+def pieces_kernel(place_ref, conv_ref, *outs):
+    for step in range(line_len):
+        outs[step][...] = conv_ref[0, place_ref[0] ^ step]
+
+
+def line_pieces(place, array):
+    chans = array.shape[2]
+    spec = pl.BlockSpec((1, line_len, chans, lane), lambda i, z: (i, 0, 0, 0))
+    return pl.pallas_call(
+        pieces_kernel,
+        grid_spec=pltpu.PrefetchScalarGridSpec(
+            num_scalar_prefetch=1,
+            grid=(quad_len,),
+            in_specs=[spec],
+            out_specs=[pl.BlockSpec((chans, lane), lambda i, z: (i, 0))] * line_len,
+        ),
+        out_shape=[jax.ShapeDtypeStruct((quad_len * chans, lane), jnp.bfloat16)] * line_len,
+        name="line_pieces",
+    )(place, array)
+
+
+def merge_columns(place, pieces, factors):
+    piece, rows = pieces[0].shape
+    spec = pl.BlockSpec((rows, piece), lambda i, z: (0, i))
+    outs = max(1, len(factors))
+
+    def kernel(place_ref, *refs):
+        parts = refs[:line_len]
+        factor_refs = refs[line_len : line_len + len(factors)]
+        out_refs = refs[line_len + len(factors) :]
+        for step in range(line_len):
+
+            @pl.when((pl.program_id(0) ^ place_ref[0]) == step)
+            def _():
+                block = parts[step][...].astype(jnp.float32).T
+                if factor_refs:
+                    for factor, out in zip(factor_refs, out_refs):
+                        out[...] = block * factor[...].astype(jnp.float32)
+                else:
+                    out_refs[0][...] = block
+
+    return pl.pallas_call(
+        kernel,
+        grid_spec=pltpu.PrefetchScalarGridSpec(
+            num_scalar_prefetch=1,
+            grid=(line_len,),
+            in_specs=[pl.BlockSpec((piece, rows), lambda i, z: (0, 0))] * line_len
+            + [spec] * len(factors),
+            out_specs=[spec] * outs,
+        ),
+        out_shape=[jax.ShapeDtypeStruct((rows, piece * line_len), jnp.float32)] * outs,
+        name="merge_columns",
+    )(place, *pieces, *factors)
+
+
+def line_exchange(pieces):
+    return [pieces[0]] + [
+        lax.ppermute(pieces[step], "line", [(i, i ^ step) for i in range(line_len)])
+        for step in range(1, line_len)
+    ]
+
+
+def line_gather(array):
+    right = [(i, i + 1) for i in range(line_len - 1)]
+    left = [(i + 1, i) for i in range(line_len - 1)]
+    lower, upper = ([], [])
+    from_lower = from_upper = array
+    for _ in range(line_len - 1):
+        from_lower = lax.ppermute(from_lower, "line", right)
+        from_upper = lax.ppermute(from_upper, "line", left)
+        lower.append(from_lower)
+        upper.append(from_upper)
+    return jnp.stack(lower[::-1] + [array] + upper)
+
+
+def quad_gather(array):
+    across = lax.ppermute(array, "quad", [(i, i ^ 2) for i in range(quad_len)])
+    row = lax.axis_index("quad") // 2
+    pair = jnp.where(row == 0, jnp.stack([array, across]), jnp.stack([across, array]))
+    other = lax.ppermute(pair, "quad", [(i, i ^ 1) for i in range(quad_len)])
+    core = lax.axis_index("quad") % 2
+    both = jnp.where(core == 0, jnp.stack([pair, other], 1), jnp.stack([other, pair], 1))
+    return both.reshape(quad_len * array.shape[0], array.shape[1])
+
+
+def quad_exchange(array):
+    return lax.all_to_all(array, "quad", split_axis=0, concat_axis=0, tiled=True)
+
+
+def per_device_line(query_proj, key_proj, value_proj, cotangent, out_weight, filters):
+    place = lax.axis_index("line").reshape(1).astype(jnp.int32)
+    chans = out_weight.shape[0]
+    cots = line_gather(cotangent)
+    weights = quad_gather(out_weight)
+    mixed_pieces = line_exchange(split_columns(place, key_proj, value_proj))
+    query_parts = line_exchange(split_columns(place, query_proj))
+    conv_tiles, corr_tiles = toeplitz_tiles(filters)
+    mixed = jnp.concatenate(
+        [piece.reshape(quad_len, 1, chans, lane) for piece in mixed_pieces], axis=1
+    )
+    mixed = quad_exchange(mixed)
+    conv = quad_exchange(convolve(place, mixed, conv_tiles))
+    grad, gated = gate(place, weights, cots, query_parts)
+    gated = quad_exchange(gated)
+    query_back = line_exchange(query_pieces(place, grad, conv))
+    mixed_grad = quad_exchange(correlate(gated, corr_tiles))
+    mixed_back = line_exchange(line_pieces(place, mixed_grad))
+    filter_grad = lag_sums(place, mixed, gated)
+    (query_grad,) = merge_columns(place, query_back, ())
+    key_grad, value_grad = merge_columns(place, mixed_back, (value_proj, key_proj))
+    return (query_grad, key_grad, value_grad, filter_grad)
+
+
 def solution(mesh):
-    placed = (
-        P(("parts", "ctx"), None),
-        P(("parts", "ctx"), None),
-        P(("parts", "ctx"), None),
-        P(("parts", "ctx"), None),
-        P("ctx", None),
-        P("ctx", None),
-    )
+    rows = P(("parts", "ctx"), None)
+    shared = P("ctx", None)
+    body = per_device_spectral
+    if mesh.shape["ctx"] == line_len * quad_len:
+        parts = mesh.shape["parts"]
+        mesh = Mesh(
+            mesh.devices.reshape(parts, line_len, quad_len), ("parts", "line", "quad")
+        )
+        rows = P(("parts", "line", "quad"), None)
+        shared = P(("line", "quad"), None)
+        body = per_device_line
     return jax.shard_map(
-        per_device,
+        body,
         mesh=mesh,
-        in_specs=placed,
-        out_specs=(
-            P(("parts", "ctx"), None),
-            P(("parts", "ctx"), None),
-            P(("parts", "ctx"), None),
-            P(("parts", "ctx"), None),
-        ),
+        in_specs=(rows, rows, rows, rows, shared, shared),
+        out_specs=(rows, rows, rows, rows),
         check_vma=False,
     )

time: 516 us -> 244 us (0.47)
  waiting for transfers between devices: 262 us -> 90 us
  Pallas kernels: 0 us -> 81.8 us
  matrix products: 70.3 us -> 0 us
  local copies, waits for them, and re-layouts: 64.6 us -> 15.8 us
  other arithmetic: 50.4 us -> 4.08 us
  between operations: 14.9 us -> 0.81 us
    all_to_all x7 -> x4, waiting for transfers between devices: 204 us -> 6.19 us  [quad_exchange(): lax.all_to_all(array, 'quad', split_axis=0, concat_axis=0, tiled=True)]
    ppermute x0 -> x20, waiting for transfers between devices: none -> 83.8 us  [the longest x12 55.2 us: line_exchange(): lax.ppermute(pieces[step], 'line', [(i, i ^ step) for i in range(line_len)])]
    pallas_call x0 -> x11, Pallas kernels: none -> 81.8 us  [the longest x1 17.3 us: lag_sums(): pl.pallas_call(lag_kernel, grid_spec=pltpu.PrefetchScalarGridSpec(num_sca...]
    dot_general x11 -> x0, matrix products: 70.3 us -> none  [the longest x5 43 us: apply_last(): jnp.einsum('qzcn,pqkn->pzck', spectrum, last_matrix(sign), precision=lax....]
    all_gather x1 -> x0, waiting for transfers between devices: 57.3 us -> none  [per_device(): lax.all_gather(out_weight, 'ctx', axis=0, tiled=True)]
    ppermute x0 -> x20, starting transfers between devices: none -> 31.3 us  [the longest x12 14.3 us: line_exchange(): lax.ppermute(pieces[step], 'line', [(i, i ^ step) for i in range(line_len)])]
    all_to_all x7 -> x4, starting transfers between devices: 46.7 us -> 17.6 us  [quad_exchange(): lax.all_to_all(array, 'quad', split_axis=0, concat_axis=0, tiled=True)]
    mul x10 -> x0, local copies, waits for them, and re-layouts: 25.4 us -> none  [the longest x7 16.2 us: channel_work(): conv_real = filt_real * mix_real - filt_imag * mix_imag]
  transfers between devices with their start and end apart: 8 -> 24, of which waited for: 6 -> 10; matrix products, arithmetic and copies ran while one was open for 15% -> 7% of each run, Pallas kernels for 0% -> 32%
where the time goes in v1:
time: 244 us; the launch traced here: 241 us
  waiting for transfers between devices  90 us (37%)
  Pallas kernels  81.8 us (34%)
  starting transfers between devices  48.9 us (20%)
  local copies, waits for them, and re-layouts  15.8 us (6%)
  other arithmetic  4.08 us (2%)
    ppermute x12, waiting for transfers between devices, line_exchange(): lax.ppermute(pieces[step], 'line', [(i, i ^ step) for i in range(line_len)])  55.2 us
    ppermute x3, waiting for transfers between devices, line_gather(): from_upper = lax.ppermute(from_upper, 'line', left)  21.6 us
    all_to_all x4, starting transfers between devices, quad_exchange(): lax.all_to_all(array, 'quad', split_axis=0, concat_axis=0, tiled=True)  17.6 us
    pallas_call x1, Pallas kernels, lag_sums(): pl.pallas_call(lag_kernel, grid_spec=pltpu.PrefetchScalarGridSpec(num_sca...  17.3 us
    ppermute x12, starting transfers between devices, line_exchange(): lax.ppermute(pieces[step], 'line', [(i, i ^ step) for i in range(line_len)])  14.3 us
    unnamed x35, local copies, waits for them, and re-layouts  14.1 us
    pallas_call x1, Pallas kernels, convolve(): pl.pallas_call(conv_kernel, grid_spec=pltpu.PrefetchScalarGridSpec(num_sc...  12.8 us
    pallas_call x1, Pallas kernels, correlate(): pl.pallas_call(corr_kernel, grid=(groups,), in_specs=[spec, pl.BlockSpec(...  12.4 us
  transfers between devices with their start and end apart: 24, of which 10 were waited for; matrix products, arithmetic and copies ran while one was open for 7% of the time, Pallas kernels for 32%

profile of v1, /device:TPU:12, one launch (start us, length us, event | category | flops | bytes accessed | tf_op | source)
XLA Modules:
  0.0 241.3 jit_solution(8557595796565108493)
XLA Ops:
  1.2 3.5 %collective-permute-start.2 = (bf16[128,2048]{1,0:T(8,128)(2,1)}, bf16[128,2048]{1,0:T(8,128)(2,1)}, u32[]{:S(2)}, u32[]{:S(2)}) collective-permute-start(bf16[128,2048]{1,0:T(8,128)(2,1)} %param.9), channel_id=1, source_target_pairs={{0,4},{4,8},{8,12},{1,5},{5,9},{9,13},{2,6},{6,10},{10,14},{3,7},{... | collective-permute-start | bytes 1572872 | tf_op jit(solution)/shard_map/ppermute | solution.py:514
  4.7 2.6 %split_columns.3 = (bf16[1024,128]{1,0:T(8,128)(2,1)}, bf16[1024,128]{1,0:T(8,128)(2,1)}, bf16[1024,128]{1,0:T(8,128)(2,1)}, bf16[1024,128]{1,0:T(8,128)(2,1)}) custom-call(s32[1]{0:T(128)} %bitcast.refs_0_.place_ref, bf16[128,4096]{1,0:T(8,128)(2,1)} %refs_5_.3, bf16[128,4096]{1,0:T(8,128)(2,1)} %refs_4_.5, bf16[128,4096]{1,0:T(8,128)(2,1)} %refs_5_.3, ...), custom_call_target="tpu_custom_call" | custom-call | tf_op jit(solution)/shard_map/split_columns/pallas_call | solution.py:190
  7.3 1.3 collective-permute-start.11
  8.6 2.7 %collective-permute-start.5 = (bf16[128,2048]{1,0:T(8,128)(2,1)}, bf16[128,2048]{1,0:T(8,128)(2,1)}, u32[]{:S(2)}, u32[]{:S(2)}) collective-permute-start(bf16[128,2048]{1,0:T(8,128)(2,1)} %param.9), channel_id=1, source_target_pairs={{4,0},{8,4},{12,8},{5,1},{9,5},{13,9},{6,2},{10,6},{14,10},{7,3},{... | collective-permute-start | bytes 1572872 | tf_op jit(solution)/shard_map/ppermute | solution.py:515
  11.3 7.0 %collective-permute-done.2 = bf16[128,2048]{1,0:T(8,128)(2,1)} collective-permute-done((bf16[128,2048]{1,0:T(8,128)(2,1)}, bf16[128,2048]{1,0:T(8,128)(2,1)}, u32[]{:S(2)}, u32[]{:S(2)}) %collective-permute-start.2) | collective-permute-done | bytes 524320 | tf_op jit(solution)/shard_map/ppermute | solution.py:514
  18.3 2.6 %collective-permute-start.3 = (bf16[128,2048]{1,0:T(8,128)(2,1)}, bf16[128,2048]{1,0:T(8,128)(2,1)}, u32[]{:S(2)}, u32[]{:S(2)}) collective-permute-start(bf16[128,2048]{1,0:T(8,128)(2,1)} %collective-permute-done.2), channel_id=1, source_target_pairs={{0,4},{4,8},{8,12},{1,5},{5,9},{9,13},{2,6},{6,10},{10,14},{3,7},{... | collective-permute-start | bytes 1572872 | tf_op jit(solution)/shard_map/ppermute | solution.py:514
  20.8 1.4 collective-permute-start.12
  22.2 1.6 collective-permute-done.11
  23.8 0.8 collective-permute-start.13
  24.5 2.3 split_columns.2
  26.9 26.3 %collective-permute-done.12 = bf16[1024,128]{1,0:T(8,128)(2,1)S(1)} collective-permute-done((bf16[1024,128]{1,0:T(8,128)(2,1)}, bf16[1024,128]{1,0:T(8,128)(2,1)S(1)}, u32[]{:S(2)}, u32[]{:S(2)}) %collective-permute-start.12) | collective-permute-done | bytes 262176 | tf_op jit(solution)/shard_map/ppermute | solution.py:503
  53.2 5.5 %collective-permute-done.13 = bf16[1024,128]{1,0:T(8,128)(2,1)S(1)} collective-permute-done((bf16[1024,128]{1,0:T(8,128)(2,1)}, bf16[1024,128]{1,0:T(8,128)(2,1)S(1)}, u32[]{:S(2)}, u32[]{:S(2)}) %collective-permute-start.13) | collective-permute-done | bytes 262176 | tf_op jit(solution)/shard_map/ppermute | solution.py:503
  58.6 1.1 pad_maximum_fusion
  59.8 5.0 %all-to-all-start = ((bf16[4,4,256,128]{3,2,1,0:T(8,128)(2,1)}), bf16[4,4,256,128]{3,2,1,0:T(8,128)(2,1)S(1)}, u32[]{:S(2)}, u32[]{:S(2)}) async-start(bf16[4,4,256,128]{3,2,1,0:T(8,128)(2,1)} %pad_maximum_fusion), calls=%async_computation | async-start | bytes 2097152 | tf_op jit(solution)/shard_map/all_to_all | solution.py:532
  64.8 3.8 %collective-permute-start.9 = (bf16[1024,128]{1,0:T(8,128)(2,1)}, bf16[1024,128]{1,0:T(8,128)(2,1)}, u32[]{:S(2)}, u32[]{:S(2)}) collective-permute-start(bf16[1024,128]{1,0:T(8,128)(2,1)} %get-tuple-element.28), channel_id=1, source_target_pairs={{0,8},{4,12},{8,0},{12,4},{1,9},{5,13},{9,1},{13,5},{2,10},{6,14},... | collective-permute-start | bytes 786440 | tf_op jit(solution)/shard_map/ppermute | solution.py:503
  68.6 1.9 collective-permute-start.6
  70.5 3.9 %collective-permute-start.4 = (bf16[128,2048]{1,0:T(8,128)(2,1)}, bf16[128,2048]{1,0:T(8,128)(2,1)S(1)}, u32[]{:S(2)}, u32[]{:S(2)}) collective-permute-start(bf16[128,2048]{1,0:T(8,128)(2,1)} %collective-permute-done.3), channel_id=1, source_target_pairs={{0,4},{4,8},{8,12},{1,5},{5,9},{9,13},{2,6},{6,10},{10,14},{3,7},{... | collective-permute-start | bytes 1572872 | tf_op jit(solution)/shard_map/ppermute | solution.py:514
  75.2 16.5 %collective-permute-done.6 = bf16[128,2048]{1,0:T(8,128)(2,1)S(1)} collective-permute-done((bf16[128,2048]{1,0:T(8,128)(2,1)}, bf16[128,2048]{1,0:T(8,128)(2,1)S(1)}, u32[]{:S(2)}, u32[]{:S(2)}) %collective-permute-start.6) | collective-permute-done | bytes 524320 | tf_op jit(solution)/shard_map/ppermute | solution.py:515
  91.7 1.9 collective-permute-start.7
  93.6 0.8 bitcast_dynamic-update-slice_fusion.6
  94.5 1.9 bitcast_dynamic-update-slice_fusion.5
  96.4 1.9 bitcast_dynamic-update-slice_fusion.4
  98.3 1.9 bitcast_dynamic-update-slice_fusion.3
  100.2 1.9 bitcast_dynamic-update-slice_fusion.2
  102.0 0.8 bitcast_dynamic-update-slice_fusion.1
  102.9 5.0 %collective-permute-done.7 = bf16[128,2048]{1,0:T(8,128)(2,1)S(1)} collective-permute-done((bf16[128,2048]{1,0:T(8,128)(2,1)S(1)}, bf16[128,2048]{1,0:T(8,128)(2,1)S(1)}, u32[]{:S(2)}, u32[]{:S(2)}) %collective-permute-start.7) | collective-permute-done | bytes 524320 | tf_op jit(solution)/shard_map/ppermute | solution.py:515
  107.9 0.9 bitcast_dynamic-update-slice_fusion.refs_0_.refs_1_.refs_2_.refs_3_
  108.8 2.3 maximum_select_fusion
  111.8 8.2 %gate.1 = (bf16[4,4,256,128]{3,2,1,0:T(8,128)(2,1)}, bf16[4,4,256,128]{3,2,1,0:T(8,128)(2,1)}) custom-call(s32[1]{0:T(128)} %bitcast.refs_0_.place_ref, bf16[1024,2048]{1,0:T(8,128)(2,1)} %bitcast.28, bf16[7,128,2048]{2,1,0:T(8,128)(2,1)} %bitcast_dynamic-update-slice_fusion.refs_0_.refs_1_.refs_2_.refs_3_, ...), custom_call_target="tpu_custom_call" | custom-call | tf_op jit(solution)/shard_map/gate/pallas_call | solution.py:408
  120.0 3.9 %all-to-all-start.2 = ((bf16[4,4,256,128]{3,2,1,0:T(8,128)(2,1)}), bf16[4,4,256,128]{3,2,1,0:T(8,128)(2,1)S(1)}, u32[]{:S(2)}, u32[]{:S(2)}) async-start(bf16[4,4,256,128]{3,2,1,0:T(8,128)(2,1)} %get-tuple-element.40), calls=%async_computation.2 | async-start | bytes 2097152 | tf_op jit(solution)/shard_map/all_to_all | solution.py:532
  123.9 0.7 reshape.98.filter_ref
  124.7 11.3 %toeplitz_tiles.1 = (bf16[16,256,1024]{2,1,0:T(8,128)(2,1)}, bf16[16,256,1024]{2,1,0:T(8,128)(2,1)}) custom-call(f32[16,1,2048]{2,1,0:T(1,128)} %reshape.98.filter_ref), custom_call_target="tpu_custom_call" | custom-call | tf_op jit(solution)/shard_map/toeplitz_tiles/pallas_call | solution.py:223
  136.0 12.8 %convolve.1 = bf16[4,4,256,128]{3,2,1,0:T(8,128)(2,1)} custom-call(s32[1]{0:T(128)} %bitcast.refs_0_.place_ref, bf16[4,4,256,128]{3,2,1,0:T(8,128)(2,1)} %copy-done, bf16[4,4,256,128]{3,2,1,0:T(8,128)(2,1)} %copy-done, bf16[4,4,256,128]{3,2,1,0:T(8,128)(2,1)} %copy-done, bf16[4,4,256,128]{3,2,1,0:T(8,128)(2,1)} %copy-done, ...), custom_call_target="tpu_custom_call" | custom-call | tf_op jit(solution)/shard_map/convolve/pallas_call | solution.py:270
  148.8 3.5 %all-to-all-start.1 = ((bf16[4,4,256,128]{3,2,1,0:T(8,128)(2,1)}), bf16[4,4,256,128]{3,2,1,0:T(8,128)(2,1)S(1)}, u32[]{:S(2)}, u32[]{:S(2)}) async-start(bf16[4,4,256,128]{3,2,1,0:T(8,128)(2,1)} %convolve.1), calls=%async_computation.1 | async-start | bytes 2097152 | tf_op jit(solution)/shard_map/all_to_all | solution.py:532
  152.3 12.4 %correlate.1 = bf16[4,4,256,128]{3,2,1,0:T(8,128)(2,1)} custom-call(bf16[4,4,256,128]{3,2,1,0:T(8,128)(2,1)} %copy-done.1, bf16[16,256,1024]{2,1,0:T(8,128)(2,1)} %get-tuple-element.41.tile_ref), custom_call_target="tpu_custom_call" | custom-call | tf_op jit(solution)/shard_map/correlate/pallas_call | solution.py:316
  165.1 5.2 %all-to-all-start.3 = ((bf16[4,4,256,128]{3,2,1,0:T(8,128)(2,1)}), bf16[4,4,256,128]{3,2,1,0:T(8,128)(2,1)S(1)}, u32[]{:S(2)}, u32[]{:S(2)}) async-start(bf16[4,4,256,128]{3,2,1,0:T(8,128)(2,1)} %correlate.1), calls=%async_computation.3 | async-start | bytes 2097152 | tf_op jit(solution)/shard_map/all_to_all | solution.py:532
  170.3 3.5 %query_pieces.1 = (bf16[1024,128]{1,0:T(8,128)(2,1)}, bf16[1024,128]{1,0:T(8,128)(2,1)}, bf16[1024,128]{1,0:T(8,128)(2,1)}, bf16[1024,128]{1,0:T(8,128)(2,1)}) custom-call(s32[1]{0:T(128)} %bitcast.refs_0_.place_ref, bf16[4,4,256,128]{3,2,1,0:T(8,128)(2,1)} %get-tuple-element.30.grad_ref, bf16[4,4,256,128]{3,2,1,0:T(8,128)(2,1)} %copy-done.3), custom_call_target="tpu_custom_call" | custom-call | tf_op jit(solution)/shard_map/query_pieces/pallas_call | solution.py:433
  174.1 2.5 %collective-permute-start.15 = (bf16[1024,128]{1,0:T(8,128)(2,1)}, bf16[1024,128]{1,0:T(8,128)(2,1)S(1)}, u32[]{:S(2)}, u32[]{:S(2)}) collective-permute-start(bf16[1024,128]{1,0:T(8,128)(2,1)} %get-tuple-element.38), channel_id=1, source_target_pairs={{0,8},{4,12},{8,0},{12,4},{1,9},{5,13},{9,1},{13,5},{2,10},{6,14},... | collective-permute-start | bytes 786440 | tf_op jit(solution)/shard_map/ppermute | solution.py:503
  177.3 5.8 %all-to-all-done.3.conv_ref = bf16[4,4,256,128]{3,2,1,0:T(8,128)(2,1)S(1)} async-done(((bf16[4,4,256,128]{3,2,1,0:T(8,128)(2,1)}), bf16[4,4,256,128]{3,2,1,0:T(8,128)(2,1)S(1)}, u32[]{:S(2)}, u32[]{:S(2)}) %all-to-all-start.3) | async-done | bytes 1048608 | tf_op jit(solution)/shard_map/all_to_all | solution.py:532
  183.1 1.0 copy-done.4
  184.0 3.4 %line_pieces.1 = (bf16[1024,128]{1,0:T(8,128)(2,1)}, bf16[1024,128]{1,0:T(8,128)(2,1)}, bf16[1024,128]{1,0:T(8,128)(2,1)}, bf16[1024,128]{1,0:T(8,128)(2,1)}) custom-call(s32[1]{0:T(128)} %bitcast.refs_0_.place_ref, bf16[4,4,256,128]{3,2,1,0:T(8,128)(2,1)} %copy-done.4), custom_call_target="tpu_custom_call" | custom-call | tf_op jit(solution)/shard_map/line_pieces/pallas_call | solution.py:454
  187.7 2.5 %collective-permute-start.18 = (bf16[1024,128]{1,0:T(8,128)(2,1)}, bf16[1024,128]{1,0:T(8,128)(2,1)S(1)}, u32[]{:S(2)}, u32[]{:S(2)}) collective-permute-start(bf16[1024,128]{1,0:T(8,128)(2,1)} %get-tuple-element.44), channel_id=1, source_target_pairs={{0,8},{4,12},{8,0},{12,4},{1,9},{5,13},{9,1},{13,5},{2,10},{6,14},... | collective-permute-start | bytes 786440 | tf_op jit(solution)/shard_map/ppermute | solution.py:503
  190.9 4.0 %collective-permute-done.15.refs_2_ = bf16[1024,128]{1,0:T(8,128)(2,1)S(1)} collective-permute-done((bf16[1024,128]{1,0:T(8,128)(2,1)}, bf16[1024,128]{1,0:T(8,128)(2,1)S(1)}, u32[]{:S(2)}, u32[]{:S(2)}) %collective-permute-start.15) | collective-permute-done | bytes 262176 | tf_op jit(solution)/shard_map/ppermute | solution.py:503
  194.9 17.9 %collective-permute-done.16.refs_3_ = bf16[1024,128]{1,0:T(8,128)(2,1)S(1)} collective-permute-done((bf16[1024,128]{1,0:T(8,128)(2,1)}, bf16[1024,128]{1,0:T(8,128)(2,1)S(1)}, u32[]{:S(2)}, u32[]{:S(2)}) %collective-permute-start.16) | collective-permute-done | bytes 262176 | tf_op jit(solution)/shard_map/ppermute | solution.py:503
  213.5 3.3 %merge_columns.2 = f32[128,4096]{1,0:T(8,128)} custom-call(s32[1]{0:T(128)} %bitcast.refs_0_.place_ref, bf16[1024,128]{1,0:T(8,128)(2,1)} %get-tuple-element.36.refs_0_, bf16[1024,128]{1,0:T(8,128)(2,1)} %copy-done.8, bf16[1024,128]{1,0:T(8,128)(2,1)} %copy-done.10, bf16[1024,128]{1,0:T(8,128)(2,1)} %copy-done.11), custom_call_target="tpu_custom_call" | custom-call | tf_op jit(solution)/shard_map/merge_columns/pallas_call | solution.py:487
  216.8 17.3 %lag_sums.1 = f32[16,1,2048]{2,1,0:T(1,128)} custom-call(s32[1]{0:T(128)} %bitcast.refs_0_.place_ref, bf16[4,4,256,128]{3,2,1,0:T(8,128)(2,1)} %copy-done, bf16[4,4,256,128]{3,2,1,0:T(8,128)(2,1)} %copy-done, bf16[4,4,256,128]{3,2,1,0:T(8,128)(2,1)} %copy-done, bf16[4,4,256,128]{3,2,1,0:T(8,128)(2,1)} %copy-done, bf16[4,4,256,128]{3,2,1,0:T(8,128)(2,1)} %copy-done.1), custom_call_target="tpu_custom_call" | custom-call | tf_op jit(solution)/shard_map/lag_sums/pallas_call | solution.py:369
  234.1 1.6 copy.12
  236.6 4.7 %merge_columns.3 = (f32[128,4096]{1,0:T(8,128)}, f32[128,4096]{1,0:T(8,128)}) custom-call(s32[1]{0:T(128)} %bitcast.refs_0_.place_ref, bf16[1024,128]{1,0:T(8,128)(2,1)} %get-tuple-element.42.refs_0_, bf16[1024,128]{1,0:T(8,128)(2,1)} %copy-done.7, bf16[1024,128]{1,0:T(8,128)(2,1)} %copy-done.9, bf16[1024,128]{1,0:T(8,128)(2,1)} %copy-done.12, ...), custom_call_target="tpu_custom_call" | custom-call | tf_op jit(solution)/shard_map/merge_columns/pallas_call | solution.py:487
  (52 shorter events, 5.9 us)
Async XLA Ops:
  0.6 68.0 %collective-permute-start = (bf16[256,2048]{1,0:T(8,128)(2,1)}, bf16[256,2048]{1,0:T(8,128)(2,1)S(1)}, u32[]{:S(2)}, u32[]{:S(2)}) collective-permute-start(bf16[256,2048]{1,0:T(8,128)(2,1)} %param.10), channel_id=1, source_target_pairs={{0,2},{1,3},{2,0},{3,1},{4,6},{5,7},{6,4},{7,5},{8,10},{9,11},{10,... | collective-permute-start | bytes 3145736 | tf_op jit(solution)/shard_map/ppermute | solution.py:522
  1.2 17.0 %collective-permute-start.2 = (bf16[128,2048]{1,0:T(8,128)(2,1)}, bf16[128,2048]{1,0:T(8,128)(2,1)}, u32[]{:S(2)}, u32[]{:S(2)}) collective-permute-start(bf16[128,2048]{1,0:T(8,128)(2,1)} %param.9), channel_id=1, source_target_pairs={{0,4},{4,8},{8,12},{1,5},{5,9},{9,13},{2,6},{6,10},{10,14},{3,7},{... | collective-permute-start | bytes 1572872 | tf_op jit(solution)/shard_map/ppermute | solution.py:514
  7.3 51.4 %copy-start.6 = (bf16[1024,128]{1,0:T(8,128)(2,1)S(1)}, bf16[1024,128]{1,0:T(8,128)(2,1)}, u32[]{:S(2)}) copy-start(bf16[1024,128]{1,0:T(8,128)(2,1)} %get-tuple-element.31) | copy-start | bytes 786436
  7.3 16.5 %collective-permute-start.11 = (bf16[1024,128]{1,0:T(8,128)(2,1)}, bf16[1024,128]{1,0:T(8,128)(2,1)S(1)}, u32[]{:S(2)}, u32[]{:S(2)}) collective-permute-start(bf16[1024,128]{1,0:T(8,128)(2,1)} %get-tuple-element.32), channel_id=1, source_target_pairs={{0,4},{4,0},{8,12},{12,8},{1,5},{5,1},{9,13},{13,9},{2,6},{6,2},{1... | collective-permute-start | bytes 786440 | tf_op jit(solution)/shard_map/ppermute | solution.py:503
  8.6 56.2 %collective-permute-start.5 = (bf16[128,2048]{1,0:T(8,128)(2,1)}, bf16[128,2048]{1,0:T(8,128)(2,1)}, u32[]{:S(2)}, u32[]{:S(2)}) collective-permute-start(bf16[128,2048]{1,0:T(8,128)(2,1)} %param.9), channel_id=1, source_target_pairs={{4,0},{8,4},{12,8},{5,1},{9,5},{13,9},{6,2},{10,6},{14,10},{7,3},{... | collective-permute-start | bytes 1572872 | tf_op jit(solution)/shard_map/ppermute | solution.py:515
  18.3 52.3 %collective-permute-start.3 = (bf16[128,2048]{1,0:T(8,128)(2,1)}, bf16[128,2048]{1,0:T(8,128)(2,1)}, u32[]{:S(2)}, u32[]{:S(2)}) collective-permute-start(bf16[128,2048]{1,0:T(8,128)(2,1)} %collective-permute-done.2), channel_id=1, source_target_pairs={{0,4},{4,8},{8,12},{1,5},{5,9},{9,13},{2,6},{6,10},{10,14},{3,7},{... | collective-permute-start | bytes 1572872 | tf_op jit(solution)/shard_map/ppermute | solution.py:514
  20.8 32.3 %collective-permute-start.12 = (bf16[1024,128]{1,0:T(8,128)(2,1)}, bf16[1024,128]{1,0:T(8,128)(2,1)S(1)}, u32[]{:S(2)}, u32[]{:S(2)}) collective-permute-start(bf16[1024,128]{1,0:T(8,128)(2,1)} %get-tuple-element.33), channel_id=1, source_target_pairs={{0,8},{4,12},{8,0},{12,4},{1,9},{5,13},{9,1},{13,5},{2,10},{6,14},... | collective-permute-start | bytes 786440 | tf_op jit(solution)/shard_map/ppermute | solution.py:503
  23.8 34.9 %collective-permute-start.13 = (bf16[1024,128]{1,0:T(8,128)(2,1)}, bf16[1024,128]{1,0:T(8,128)(2,1)S(1)}, u32[]{:S(2)}, u32[]{:S(2)}) collective-permute-start(bf16[1024,128]{1,0:T(8,128)(2,1)} %get-tuple-element.34), channel_id=1, source_target_pairs={{0,12},{4,8},{8,4},{12,0},{1,13},{5,9},{9,5},{13,1},{2,14},{6,10},... | collective-permute-start | bytes 786440 | tf_op jit(solution)/shard_map/ppermute | solution.py:503
  24.5 49.9 %copy-start.2 = (bf16[256,2048]{1,0:T(8,128)(2,1)S(1)}, bf16[256,2048]{1,0:T(8,128)(2,1)}, u32[]{:S(2)}) copy-start(bf16[256,2048]{1,0:T(8,128)(2,1)} %param.10) | copy-start | bytes 3145732
  53.2 57.9 %collective-permute-start.10 = (bf16[1024,128]{1,0:T(8,128)(2,1)}, bf16[1024,128]{1,0:T(8,128)(2,1)S(1)}, u32[]{:S(2)}, u32[]{:S(2)}) collective-permute-start(bf16[1024,128]{1,0:T(8,128)(2,1)} %get-tuple-element.29), channel_id=1, source_target_pairs={{0,12},{4,8},{8,4},{12,0},{1,13},{5,9},{9,5},{13,1},{2,14},{6,10},... | collective-permute-start | bytes 786440 | tf_op jit(solution)/shard_map/ppermute | solution.py:503
  58.6 52.5 %collective-permute-start.8 = (bf16[1024,128]{1,0:T(8,128)(2,1)}, bf16[1024,128]{1,0:T(8,128)(2,1)}, u32[]{:S(2)}, u32[]{:S(2)}) collective-permute-start(bf16[1024,128]{1,0:T(8,128)(2,1)} %get-tuple-element.27), channel_id=1, source_target_pairs={{0,4},{4,0},{8,12},{12,8},{1,5},{5,1},{9,13},{13,9},{2,6},{6,2},{1... | collective-permute-start | bytes 786440 | tf_op jit(solution)/shard_map/ppermute | solution.py:503
  59.8 60.3 %all-to-all-start = ((bf16[4,4,256,128]{3,2,1,0:T(8,128)(2,1)}), bf16[4,4,256,128]{3,2,1,0:T(8,128)(2,1)S(1)}, u32[]{:S(2)}, u32[]{:S(2)}) async-start(bf16[4,4,256,128]{3,2,1,0:T(8,128)(2,1)} %pad_maximum_fusion), calls=%async_computation | async-start | bytes 2097152 | tf_op jit(solution)/shard_map/all_to_all | solution.py:532
  64.8 46.4 %collective-permute-start.9 = (bf16[1024,128]{1,0:T(8,128)(2,1)}, bf16[1024,128]{1,0:T(8,128)(2,1)}, u32[]{:S(2)}, u32[]{:S(2)}) collective-permute-start(bf16[1024,128]{1,0:T(8,128)(2,1)} %get-tuple-element.28), channel_id=1, source_target_pairs={{0,8},{4,12},{8,0},{12,4},{1,9},{5,13},{9,1},{13,5},{2,10},{6,14},... | collective-permute-start | bytes 786440 | tf_op jit(solution)/shard_map/ppermute | solution.py:503
  68.6 23.1 %collective-permute-start.6 = (bf16[128,2048]{1,0:T(8,128)(2,1)}, bf16[128,2048]{1,0:T(8,128)(2,1)S(1)}, u32[]{:S(2)}, u32[]{:S(2)}) collective-permute-start(bf16[128,2048]{1,0:T(8,128)(2,1)} %collective-permute-done.5), channel_id=1, source_target_pairs={{4,0},{8,4},{12,8},{5,1},{9,5},{13,9},{6,2},{10,6},{14,10},{7,3},{... | collective-permute-start | bytes 1572872 | tf_op jit(solution)/shard_map/ppermute | solution.py:515
  70.5 21.2 %collective-permute-start.4 = (bf16[128,2048]{1,0:T(8,128)(2,1)}, bf16[128,2048]{1,0:T(8,128)(2,1)S(1)}, u32[]{:S(2)}, u32[]{:S(2)}) collective-permute-start(bf16[128,2048]{1,0:T(8,128)(2,1)} %collective-permute-done.3), channel_id=1, source_target_pairs={{0,4},{4,8},{8,12},{1,5},{5,9},{9,13},{2,6},{6,10},{10,14},{3,7},{... | collective-permute-start | bytes 1572872 | tf_op jit(solution)/shard_map/ppermute | solution.py:514
  91.7 17.1 %collective-permute-start.1 = (bf16[2,256,2048]{2,1,0:T(8,128)(2,1)S(1)}, bf16[2,256,2048]{2,1,0:T(8,128)(2,1)S(1)}, u32[]{:S(2)}, u32[]{:S(2)}) collective-permute-start(bf16[2,256,2048]{2,1,0:T(8,128)(2,1)S(1)} %maximum_select_fusion.2), channel_id=1, source_target_pairs={{0,1},{1,0},{2,3},{3,2},{4,5},{5,4},{6,7},{7,6},{8,9},{9,8},{10,11... | collective-permute-start | bytes 6291464 | tf_op jit(solution)/shard_map/ppermute | solution.py:525
  91.7 16.2 %collective-permute-start.7 = (bf16[128,2048]{1,0:T(8,128)(2,1)S(1)}, bf16[128,2048]{1,0:T(8,128)(2,1)S(1)}, u32[]{:S(2)}, u32[]{:S(2)}) collective-permute-start(bf16[128,2048]{1,0:T(8,128)(2,1)S(1)} %collective-permute-done.6), channel_id=1, source_target_pairs={{4,0},{8,4},{12,8},{5,1},{9,5},{13,9},{6,2},{10,6},{14,10},{7,3},{... | collective-permute-start | bytes 1572872 | tf_op jit(solution)/shard_map/ppermute | solution.py:515
  111.1 0.7 copy-start.5
  111.8 12.1 %copy-start.13 = (f32[16,2048]{1,0:T(8,128)S(1)}, f32[16,2048]{1,0:T(8,128)}, u32[]{:S(2)}) copy-start(f32[16,2048]{1,0:T(8,128)} %param.11) | copy-start | bytes 393220
  120.0 16.0 %copy-start = (bf16[4,4,256,128]{3,2,1,0:T(8,128)(2,1)}, bf16[4,4,256,128]{3,2,1,0:T(8,128)(2,1)S(1)}, u32[]{:S(2)}) copy-start(bf16[4,4,256,128]{3,2,1,0:T(8,128)(2,1)S(1)} %all-to-all-done.refs_0_.refs_1_.refs_2_.refs_3_) | copy-start | bytes 3145732
  120.0 28.8 %all-to-all-start.2 = ((bf16[4,4,256,128]{3,2,1,0:T(8,128)(2,1)}), bf16[4,4,256,128]{3,2,1,0:T(8,128)(2,1)S(1)}, u32[]{:S(2)}, u32[]{:S(2)}) async-start(bf16[4,4,256,128]{3,2,1,0:T(8,128)(2,1)} %get-tuple-element.40), calls=%async_computation.2 | async-start | bytes 2097152 | tf_op jit(solution)/shard_map/all_to_all | solution.py:532
  148.8 3.6 %copy-start.1 = (bf16[4,4,256,128]{3,2,1,0:T(8,128)(2,1)}, bf16[4,4,256,128]{3,2,1,0:T(8,128)(2,1)S(1)}, u32[]{:S(2)}) copy-start(bf16[4,4,256,128]{3,2,1,0:T(8,128)(2,1)S(1)} %all-to-all-done.2.gated_ref.refs_4_) | copy-start | bytes 3145732
  148.8 16.3 %all-to-all-start.1 = ((bf16[4,4,256,128]{3,2,1,0:T(8,128)(2,1)}), bf16[4,4,256,128]{3,2,1,0:T(8,128)(2,1)S(1)}, u32[]{:S(2)}, u32[]{:S(2)}) async-start(bf16[4,4,256,128]{3,2,1,0:T(8,128)(2,1)} %convolve.1), calls=%async_computation.1 | async-start | bytes 2097152 | tf_op jit(solution)/shard_map/all_to_all | solution.py:532
  165.1 5.2 %copy-start.3 = (bf16[4,4,256,128]{3,2,1,0:T(8,128)(2,1)}, bf16[4,4,256,128]{3,2,1,0:T(8,128)(2,1)S(1)}, u32[]{:S(2)}) copy-start(bf16[4,4,256,128]{3,2,1,0:T(8,128)(2,1)S(1)} %all-to-all-done.1.conv_ref) | copy-start | bytes 3145732
  165.1 18.0 %all-to-all-start.3 = ((bf16[4,4,256,128]{3,2,1,0:T(8,128)(2,1)}), bf16[4,4,256,128]{3,2,1,0:T(8,128)(2,1)S(1)}, u32[]{:S(2)}, u32[]{:S(2)}) async-start(bf16[4,4,256,128]{3,2,1,0:T(8,128)(2,1)} %correlate.1), calls=%async_computation.3 | async-start | bytes 2097152 | tf_op jit(solution)/shard_map/all_to_all | solution.py:532
  173.8 16.4 %collective-permute-start.14 = (bf16[1024,128]{1,0:T(8,128)(2,1)}, bf16[1024,128]{1,0:T(8,128)(2,1)S(1)}, u32[]{:S(2)}, u32[]{:S(2)}) collective-permute-start(bf16[1024,128]{1,0:T(8,128)(2,1)} %get-tuple-element.37), channel_id=1, source_target_pairs={{0,4},{4,0},{8,12},{12,8},{1,5},{5,1},{9,13},{13,9},{2,6},{6,2},{1... | collective-permute-start | bytes 786440 | tf_op jit(solution)/shard_map/ppermute | solution.py:503
  174.1 20.8 %collective-permute-start.15 = (bf16[1024,128]{1,0:T(8,128)(2,1)}, bf16[1024,128]{1,0:T(8,128)(2,1)S(1)}, u32[]{:S(2)}, u32[]{:S(2)}) collective-permute-start(bf16[1024,128]{1,0:T(8,128)(2,1)} %get-tuple-element.38), channel_id=1, source_target_pairs={{0,8},{4,12},{8,0},{12,4},{1,9},{5,13},{9,1},{13,5},{2,10},{6,14},... | collective-permute-start | bytes 786440 | tf_op jit(solution)/shard_map/ppermute | solution.py:503
  176.6 36.2 %collective-permute-start.16 = (bf16[1024,128]{1,0:T(8,128)(2,1)}, bf16[1024,128]{1,0:T(8,128)(2,1)S(1)}, u32[]{:S(2)}, u32[]{:S(2)}) collective-permute-start(bf16[1024,128]{1,0:T(8,128)(2,1)} %get-tuple-element.39), channel_id=1, source_target_pairs={{0,12},{4,8},{8,4},{12,0},{1,13},{5,9},{9,5},{13,1},{2,14},{6,10},... | collective-permute-start | bytes 786440 | tf_op jit(solution)/shard_map/ppermute | solution.py:503
  183.1 1.0 copy-start.4
  187.4 48.3 %collective-permute-start.17 = (bf16[1024,128]{1,0:T(8,128)(2,1)}, bf16[1024,128]{1,0:T(8,128)(2,1)S(1)}, u32[]{:S(2)}, u32[]{:S(2)}) collective-permute-start(bf16[1024,128]{1,0:T(8,128)(2,1)} %get-tuple-element.43), channel_id=1, source_target_pairs={{0,4},{4,0},{8,12},{12,8},{1,5},{5,1},{9,13},{13,9},{2,6},{6,2},{1... | collective-permute-start | bytes 786440 | tf_op jit(solution)/shard_map/ppermute | solution.py:503
  187.7 48.0 %collective-permute-start.18 = (bf16[1024,128]{1,0:T(8,128)(2,1)}, bf16[1024,128]{1,0:T(8,128)(2,1)S(1)}, u32[]{:S(2)}, u32[]{:S(2)}) collective-permute-start(bf16[1024,128]{1,0:T(8,128)(2,1)} %get-tuple-element.44), channel_id=1, source_target_pairs={{0,8},{4,12},{8,0},{12,4},{1,9},{5,13},{9,1},{13,5},{2,10},{6,14},... | collective-permute-start | bytes 786440 | tf_op jit(solution)/shard_map/ppermute | solution.py:503
  190.2 22.6 %copy-start.8 = (bf16[1024,128]{1,0:T(8,128)(2,1)}, bf16[1024,128]{1,0:T(8,128)(2,1)S(1)}, u32[]{:S(2)}) copy-start(bf16[1024,128]{1,0:T(8,128)(2,1)S(1)} %collective-permute-done.14.refs_1_) | copy-start | bytes 786436
  190.2 45.5 %collective-permute-start.19 = (bf16[1024,128]{1,0:T(8,128)(2,1)}, bf16[1024,128]{1,0:T(8,128)(2,1)S(1)}, u32[]{:S(2)}, u32[]{:S(2)}) collective-permute-start(bf16[1024,128]{1,0:T(8,128)(2,1)} %get-tuple-element.45), channel_id=1, source_target_pairs={{0,12},{4,8},{8,4},{12,0},{1,13},{5,9},{9,5},{13,1},{2,14},{6,10},... | collective-permute-start | bytes 786440 | tf_op jit(solution)/shard_map/ppermute | solution.py:503
  194.9 17.9 %copy-start.10 = (bf16[1024,128]{1,0:T(8,128)(2,1)}, bf16[1024,128]{1,0:T(8,128)(2,1)S(1)}, u32[]{:S(2)}) copy-start(bf16[1024,128]{1,0:T(8,128)(2,1)S(1)} %collective-permute-done.15.refs_2_) | copy-start | bytes 786436
  212.8 0.7 copy-start.11
  235.7 0.7 copy-start.7
  235.7 0.8 copy-start.9
  235.7 0.9 copy-start.12
